TPU v7x, 512 devices: a whole 4x4x16 slice. The times are simulated.
512 devices in a mesh: mode: 32 (over x_hi, z), slab: 16 (over x_lo, y, core).
Axes of the slice: x: 4 (x_hi: 2, x_lo: 2; x = x_hi * 2 + x_lo), y: 4, z: 16, core: 2. Of those that a mesh axis runs over, the one named last changes fastest.
Arguments:
- rhs: float32 [256, 5, 512, 128], P('mode', None, 'slab'), may hold values from -6 to 6
- start_state: float32 [256, 5, 512, 128], P('mode', None, 'slab'), may hold values from -6 to 6
- precond: bfloat16 [2, 5, 512, 5, 32], P(None, None, 'slab')
- coupling: float32 [2, 8, 5, 512], P(None, None, None, 'slab'), may hold values from -0.9 to 0.9
- edge_coef: float32 [5, 512], P(None, 'slab'), may hold values from 0.7 to 1.4
- harm_order: int32 [8], replicated, may hold values from 0 to 7, each once
Outputs:
- state: float32 [256, 5, 512, 128], P('mode', None, 'slab')
Inputs may be any that keep to these rules, and one draw needn't show every extreme that they name: harm_order holds each of 0 to 7 once.
All inputs are finite; a program needn't handle non-finite values.
Results may differ from a plain program's by a relative error of at most 0.0037.
Values may be sent and summed in bfloat16 or wider, within the bound.
A program may use at most 64 MiB of HBM per device.

v0:
```python
import jax
import jax.numpy as jnp
from jax import lax
from jax.sharding import PartitionSpec as P

NH = 8
HSTEP = 6
ITERS = 2


def passed_along(value, axis, steps):
    count = lax.axis_size(axis)
    first, last = (max(0, -steps), min(count, count - steps))
    return lax.ppermute(value, axis, [(source, source + steps) for source in range(first, last)])


def prefix_2(value, axis, join, neutral):
    count, mine = (lax.axis_size(axis), lax.axis_index(axis))
    pieces = jax.tree.map(lambda part: lax.all_gather(part, axis), value)
    running = jax.tree.map(
        lambda part, zero: jnp.full_like(part, 0) + jnp.asarray(zero, part.dtype), value, neutral
    )

    def step(position, running):
        longer = join(running, jax.tree.map(lambda part: part[position], pieces))
        return jax.tree.map(lambda new, old: jnp.where(position < mine, new, old), longer, running)

    return lax.fori_loop(0, count - 1, step, running)


def complex_scale(coef, field):
    half_cols = field.shape[-1] // 2
    coef_real = coef[0][None, :, :, None]
    coef_imag = coef[1][None, :, :, None]
    field_real = field[..., :half_cols]
    field_imag = field[..., half_cols:]
    return jnp.concatenate(
        [
            coef_real * field_real - coef_imag * field_imag,
            coef_real * field_imag + coef_imag * field_real,
        ],
        axis=-1,
    )


def complex_apply(block, field):
    half_cols = field.shape[-1] // 2
    swapped = jnp.concatenate([-field[..., half_cols:], field[..., :half_cols]], axis=-1)
    stacked = jnp.stack([field, swapped], axis=0)
    return jnp.einsum("avrwt,amwtc->mvrc", block, stacked, preferred_element_type=jnp.float32)


def column_apply(column, pushed):
    half_cols = pushed.shape[-1] // 2
    push_real = pushed[..., :half_cols]
    push_imag = pushed[..., half_cols:]
    high = lax.Precision.HIGHEST
    real_part = jnp.einsum("vrw,mwc->mvrc", column[0], push_real, precision=high) - jnp.einsum(
        "vrw,mwc->mvrc", column[1], push_imag, precision=high
    )
    imag_part = jnp.einsum("vrw,mwc->mvrc", column[0], push_imag, precision=high) + jnp.einsum(
        "vrw,mwc->mvrc", column[1], push_real, precision=high
    )
    return jnp.concatenate([real_part, imag_part], axis=-1)


def edge_mix(map_real, map_imag, vector):
    half_cols = vector.shape[-1] // 2
    vec_real = vector[..., :half_cols]
    vec_imag = vector[..., half_cols:]
    high = lax.Precision.HIGHEST
    real_part = jnp.einsum("vw,mwc->mvc", map_real, vec_real, precision=high) - jnp.einsum(
        "vw,mwc->mvc", map_imag, vec_imag, precision=high
    )
    imag_part = jnp.einsum("vw,mwc->mvc", map_real, vec_imag, precision=high) + jnp.einsum(
        "vw,mwc->mvc", map_imag, vec_real, precision=high
    )
    return jnp.concatenate([real_part, imag_part], axis=-1)


def compose(earlier, later):
    high = lax.Precision.HIGHEST
    first_real, first_imag, first_shift = earlier
    second_real, second_imag, second_shift = later
    joined_real = jnp.dot(second_real, first_real, precision=high) - jnp.dot(
        second_imag, first_imag, precision=high
    )
    joined_imag = jnp.dot(second_real, first_imag, precision=high) + jnp.dot(
        second_imag, first_real, precision=high
    )
    joined_shift = edge_mix(second_real, second_imag, first_shift) + second_shift
    return (joined_real, joined_imag, joined_shift)


def body(rhs, start_state, precond, coupling, edge_coef, harm_order):
    mode_count = rhs.shape[0]
    var_count = rhs.shape[1]
    reach = HSTEP * NH // 2
    hops = -(-reach // mode_count)
    half_harm = NH // 2
    offsets = jnp.where(
        harm_order < half_harm,
        HSTEP * (harm_order - half_harm),
        HSTEP * (harm_order - half_harm + 1),
    )
    first_gain = edge_coef[:, 0]
    last_gain = edge_coef[:, -1]
    column = precond[:, :, :, :, 0].astype(jnp.float32)
    transfer = -column[:, :, -1, :] * first_gain[None, None, :]
    state = start_state
    for outer in range(ITERS):
        frozen = state.astype(jnp.bfloat16)
        lower_list = []
        upper_list = []
        for direction in (1, -1):
            for hop in range(1, hops + 1):
                moved = passed_along(frozen, "mode", direction * hop)
                if direction == 1:
                    lower_list.append(moved)
                else:
                    upper_list.append(moved)
        extended = jnp.concatenate(lower_list[::-1] + [frozen] + upper_list, axis=0)
        mixing = jnp.zeros(state.shape, jnp.float32)
        for index in range(NH):
            begin = hops * mode_count - offsets[index]
            partner = lax.dynamic_slice_in_dim(extended, begin, mode_count, 0)
            mixing = mixing + complex_scale(coupling[:, index], partner.astype(jnp.float32))
        forced = complex_apply(precond, mixing.astype(jnp.bfloat16))
        next_row = passed_along(state[:, :, 0, :], "slab", -1)
        last_row = rhs[:, :, -1, :] + last_gain[None, :, None] * next_row
        sweep_in = jnp.concatenate([rhs[:, :, :-1, :], last_row[:, :, None, :]], axis=2).astype(
            jnp.bfloat16
        )
        local = complex_apply(precond, sweep_in) - forced
        tail = local[:, :, -1, :]
        identity = (
            jnp.eye(var_count, dtype=jnp.float32),
            jnp.zeros((var_count, var_count), jnp.float32),
            jnp.zeros_like(tail),
        )
        prefix = prefix_2((transfer[0], transfer[1], tail), "slab", compose, identity)
        carried = prefix[2]
        pushed = first_gain[None, :, None] * carried
        state = local - column_apply(column, pushed)
    return state


def solution(mesh):
    in_specs = (
        P("mode", None, "slab", None),
        P("mode", None, "slab", None),
        P(None, None, "slab", None, None),
        P(None, None, None, "slab"),
        P(None, "slab"),
        P(),
    )
    out_specs = P("mode", None, "slab", None)
    return jax.shard_map(body, mesh=mesh, in_specs=in_specs, out_specs=out_specs, check_vma=False)
```

profile of v0, /device:TPU:33, one launch (start us, length us, event | category | flops | bytes accessed | tf_op | source)
XLA Modules:
  0.0 267.9 jit_solution(373737561661215899)
XLA Ops:
  0.0 1.9 convert_element_type.98
  2.0 8.2 %collective-permute-start.1 = (bf16[8,5,32,128]{3,2,1,0:T(8,128)(2,1)}, bf16[8,5,32,128]{3,2,1,0:T(8,128)(2,1)}, u32[]{:S(2)}, u32[]{:S(2)}) collective-permute-start(bf16[8,5,32,128]{3,2,1,0:T(8,128)(2,1)} %convert_element_type.98), channel_id=1, source_target_pairs={{0,48},{16,64},{32,80},{48,96},{64,112},{80,128},{96,144},{112,160... | collective-permute-start | bytes 983048 | tf_op jit(solution)/shard_map/ppermute | solution.py:14
  10.1 4.9 %collective-permute-start.2 = (bf16[8,5,32,128]{3,2,1,0:T(8,128)(2,1)}, bf16[8,5,32,128]{3,2,1,0:T(8,128)(2,1)}, u32[]{:S(2)}, u32[]{:S(2)}) collective-permute-start(bf16[8,5,32,128]{3,2,1,0:T(8,128)(2,1)} %convert_element_type.98), channel_id=1, source_target_pairs={{0,32},{16,48},{32,64},{48,80},{64,96},{80,112},{96,128},{112,144}... | collective-permute-start | bytes 983048 | tf_op jit(solution)/shard_map/ppermute | solution.py:14
  15.0 2.8 %collective-permute-start.3 = (bf16[8,5,32,128]{3,2,1,0:T(8,128)(2,1)}, bf16[8,5,32,128]{3,2,1,0:T(8,128)(2,1)S(1)}, u32[]{:S(2)}, u32[]{:S(2)}) collective-permute-start(bf16[8,5,32,128]{3,2,1,0:T(8,128)(2,1)} %convert_element_type.98), channel_id=1, source_target_pairs={{0,16},{16,32},{32,48},{48,64},{64,80},{80,96},{96,112},{112,128},... | collective-permute-start | bytes 983048 | tf_op jit(solution)/shard_map/ppermute | solution.py:14
  17.9 2.5 collective-permute-start.4
  20.3 0.9 slice.366
  21.3 3.7 %collective-permute-start = (f32[8,5,128]{2,0,1:T(8,128)S(1)}, f32[8,5,128]{2,0,1:T(8,128)S(1)}, u32[]{:S(2)}, u32[]{:S(2)}) collective-permute-start(f32[8,5,128]{2,0,1:T(8,128)S(1)} %bitcast.379), channel_id=1, source_target_pairs={{1,0},{2,1},{3,2},{4,3},{5,4},{6,5},{7,6},{8,7},{9,8},{10,9},{11,1... | collective-permute-start | bytes 61448 | tf_op jit(solution)/shard_map/ppermute | solution.py:14
  25.0 0.7 compare_select_fusion
  25.7 1.3 fusion.115
  26.9 1.0 slice_reduce_fusion
  27.9 1.1 slice_bitcast_fusion.12
  29.0 1.1 fusion.114
  30.1 2.0 copy.421
  32.1 0.7 fusion.117
  42.8 0.3 copy.442
  43.1 0.3 copy.443
  43.5 20.0 %all_gather.14 = f32[16,5,5]{2,1,0:T(8,128)S(1)} all-gather(f32[1,5,5]{2,1,0:T(8,128)S(1)} %copy.396), channel_id=1, replica_groups=mesh['mode'=32,'slab'=16] {'slab'}, dimensions={0}, use_global_device_ids=true | all-gather | bytes 1700 | tf_op jit(solution)/shard_map/all_gather | solution.py:19
  63.5 16.4 %all_gather.15 = f32[16,5,5]{2,1,0:T(8,128)S(1)} all-gather(f32[1,5,5]{2,1,0:T(8,128)S(1)} %copy.397), channel_id=1, replica_groups=mesh['mode'=32,'slab'=16] {'slab'}, dimensions={0}, use_global_device_ids=true | all-gather | bytes 1700 | tf_op jit(solution)/shard_map/all_gather | solution.py:19
  79.9 1.3 collective-permute-start.5
  81.9 1.3 collective-permute-start.6
  83.2 1.0 constant_dynamic-update-slice_fusion.6
  84.2 1.0 constant_dynamic-update-slice_fusion.5
  85.4 10.2 %collective-permute-done.5 = bf16[8,5,32,128]{3,2,1,0:T(8,128)(2,1)S(1)} collective-permute-done((bf16[8,5,32,128]{3,2,1,0:T(8,128)(2,1)}, bf16[8,5,32,128]{3,2,1,0:T(8,128)(2,1)S(1)}, u32[]{:S(2)}, u32[]{:S(2)}) %collective-permute-start.5) | collective-permute-done | bytes 327712 | tf_op jit(solution)/shard_map/ppermute | solution.py:14
  95.7 27.0 %collective-permute-done.6 = bf16[8,5,32,128]{3,2,1,0:T(8,128)(2,1)S(1)} collective-permute-done((bf16[8,5,32,128]{3,2,1,0:T(8,128)(2,1)}, bf16[8,5,32,128]{3,2,1,0:T(8,128)(2,1)S(1)}, u32[]{:S(2)}, u32[]{:S(2)}) %collective-permute-start.6) | collective-permute-done | bytes 327712 | tf_op jit(solution)/shard_map/ppermute | solution.py:14
  122.7 0.8 dynamic-slice_convert_fusion.8
  123.5 0.6 multiply_subtract_fusion.8
  124.1 0.5 multiply_subtract_fusion.10
  124.6 0.5 multiply_subtract_fusion.12
  125.2 0.6 multiply_subtract_fusion.14
  125.7 1.4 fusion.63
  127.5 1.4 fusion.56
  128.9 0.4 convolution_bitcast_fusion.1
  129.3 0.4 fusion.47
  129.8 19.5 %all-gather = f32[128,5,1,128]{3,2,1,0:T(1,128)S(1)} all-gather(f32[8,5,1,128]{3,2,1,0:T(1,128)S(1)} %slice.477), channel_id=2, replica_groups=mesh['mode'=32,'slab'=16] {'slab'}, dimensions={0}, use_global_device_ids=true | all-gather | bytes 348160 | tf_op jit(solution)/shard_map/all_gather | solution.py:19
  149.3 13.7 %while.28 = (s32[]{:T(128)}, f32[8,5,128]{2,1,0:T(8,128)S(1)}, s32[]{:T(128)}, f32[16,5,5]{2,1,0:T(8,128)S(1)}, f32[16,5,5]{2,1,0:T(8,128)S(1)}, /*index=5*/f32[16,8,5,128]{3,2,1,0:T(8,128)S(1)}, s32[]{:T(128)}, s32[]{:T(128)}) while((s32[]{:T(128)}, f32[8,5,128]{2,1,0:T(8,128)S(1)}, s32[]{:T(128)}, f32[16,5,5]{2,1,0:T(8,128)S(1)}, ...), condition=%wide.region_1.2_spmd.clone, body=%wide.region_0.1_spmd.clone.sunk | while | flops 645124 | bytes 376958 | solution.py:28
  163.1 0.5 fusion.97
  163.5 0.5 fusion.98
  164.0 0.5 fusion.45
  164.5 0.5 fusion.44
  165.3 2.1 collective-permute-start.7
  167.4 3.7 %collective-permute-start.8 = (bf16[8,5,32,128]{3,2,1,0:T(8,128)(2,1)S(1)}, bf16[8,5,32,128]{3,2,1,0:T(8,128)(2,1)S(1)}, u32[]{:S(2)}, u32[]{:S(2)}) collective-permute-start(bf16[8,5,32,128]{3,2,1,0:T(8,128)(2,1)S(1)} %get-tuple-element.389), channel_id=1, source_target_pairs={{0,48},{16,64},{32,80},{48,96},{64,112},{80,128},{96,144},{112,160... | collective-permute-start | bytes 983048 | tf_op jit(solution)/shard_map/ppermute | solution.py:14
  171.1 4.4 %collective-permute-start.9 = (bf16[8,5,32,128]{3,2,1,0:T(8,128)(2,1)S(1)}, bf16[8,5,32,128]{3,2,1,0:T(8,128)(2,1)S(1)}, u32[]{:S(2)}, u32[]{:S(2)}) collective-permute-start(bf16[8,5,32,128]{3,2,1,0:T(8,128)(2,1)S(1)} %get-tuple-element.389), channel_id=1, source_target_pairs={{0,32},{16,48},{32,64},{48,80},{64,96},{80,112},{96,128},{112,144}... | collective-permute-start | bytes 983048 | tf_op jit(solution)/shard_map/ppermute | solution.py:14
  175.5 1.9 collective-permute-start.10
  177.5 3.3 %collective-permute-start.11 = (bf16[8,5,32,128]{3,2,1,0:T(8,128)(2,1)S(1)}, bf16[8,5,32,128]{3,2,1,0:T(8,128)(2,1)S(1)}, u32[]{:S(2)}, u32[]{:S(2)}) collective-permute-start(bf16[8,5,32,128]{3,2,1,0:T(8,128)(2,1)S(1)} %get-tuple-element.389), channel_id=1, source_target_pairs={{16,0},{32,16},{48,32},{64,48},{80,64},{96,80},{112,96},{128,112},... | collective-permute-start | bytes 983048 | tf_op jit(solution)/shard_map/ppermute | solution.py:14
  180.8 1.3 collective-permute-start.12
  182.7 0.4 fusion.66
  183.1 13.2 %collective-permute-done.8 = bf16[8,5,32,128]{3,2,1,0:T(8,128)(2,1)S(1)} collective-permute-done((bf16[8,5,32,128]{3,2,1,0:T(8,128)(2,1)S(1)}, bf16[8,5,32,128]{3,2,1,0:T(8,128)(2,1)S(1)}, u32[]{:S(2)}, u32[]{:S(2)}) %collective-permute-start.8) | collective-permute-done | bytes 327712 | tf_op jit(solution)/shard_map/ppermute | solution.py:14
  196.2 1.3 collective-permute-start.13
  197.6 9.3 %collective-permute-done.9 = bf16[8,5,32,128]{3,2,1,0:T(8,128)(2,1)S(1)} collective-permute-done((bf16[8,5,32,128]{3,2,1,0:T(8,128)(2,1)S(1)}, bf16[8,5,32,128]{3,2,1,0:T(8,128)(2,1)S(1)}, u32[]{:S(2)}, u32[]{:S(2)}) %collective-permute-start.9) | collective-permute-done | bytes 327712 | tf_op jit(solution)/shard_map/ppermute | solution.py:14
  206.9 8.8 %collective-permute-done.10 = bf16[8,5,32,128]{3,2,1,0:T(8,128)(2,1)S(1)} collective-permute-done((bf16[8,5,32,128]{3,2,1,0:T(8,128)(2,1)S(1)}, bf16[8,5,32,128]{3,2,1,0:T(8,128)(2,1)S(1)}, u32[]{:S(2)}, u32[]{:S(2)}) %collective-permute-start.10) | collective-permute-done | bytes 327712 | tf_op jit(solution)/shard_map/ppermute | solution.py:14
  215.9 10.0 %collective-permute-done.13 = bf16[8,5,32,128]{3,2,1,0:T(8,128)(2,1)S(1)} collective-permute-done((bf16[8,5,32,128]{3,2,1,0:T(8,128)(2,1)S(1)}, bf16[8,5,32,128]{3,2,1,0:T(8,128)(2,1)S(1)}, u32[]{:S(2)}, u32[]{:S(2)}) %collective-permute-start.13) | collective-permute-done | bytes 327712 | tf_op jit(solution)/shard_map/ppermute | solution.py:14
  226.0 0.8 dynamic-slice_convert_fusion
  226.7 0.3 multiply_subtract_fusion.4
  227.0 0.3 multiply_subtract_fusion.3
  229.2 1.4 fusion.84
  231.0 1.4 fusion.77
  232.4 0.4 convolution_bitcast_fusion
  232.9 18.1 %all-gather.1 = f32[128,5,1,128]{3,2,1,0:T(1,128)S(1)} all-gather(f32[8,5,1,128]{3,2,1,0:T(1,128)S(1)} %slice.501), channel_id=3, replica_groups=mesh['mode'=32,'slab'=16] {'slab'}, dimensions={0}, use_global_device_ids=true | all-gather | bytes 348160 | tf_op jit(solution)/shard_map/all_gather | solution.py:19
  251.0 13.7 %while.29 = (s32[]{:T(128)}, f32[8,5,128]{2,1,0:T(8,128)S(1)}, s32[]{:T(128)}, f32[16,5,5]{2,1,0:T(8,128)S(1)}, f32[16,5,5]{2,1,0:T(8,128)S(1)}, /*index=5*/f32[16,8,5,128]{3,2,1,0:T(8,128)S(1)}, s32[]{:T(128)}, s32[]{:T(128)}) while((s32[]{:T(128)}, f32[8,5,128]{2,1,0:T(8,128)S(1)}, s32[]{:T(128)}, f32[16,5,5]{2,1,0:T(8,128)S(1)}, ...), condition=%wide.region_3.4_spmd.clone, body=%wide.region_2.3_spmd.clone.sunk | while | flops 645124 | bytes 376958 | solution.py:28
  264.8 0.5 fusion.99
  265.3 0.5 fusion.100
  265.8 0.5 fusion.43
  266.3 0.5 fusion.42
  266.8 1.1 maximum_subtract_fusion.1
  (262 shorter events, 31.6 us)
Async XLA Ops:
  0.0 42.5 %copy-start.2 = (f32[8,5,32,128]{3,2,1,0:T(8,128)S(1)}, f32[8,5,32,128]{3,2,1,0:T(8,128)}, u32[]{:S(2)}) copy-start(f32[8,5,32,128]{3,2,1,0:T(8,128)} %param.10) | copy-start | bytes 1966084
  0.0 30.1 %copy-start.1 = (bf16[2,5,32,5,32]{4,2,3,1,0:T(8,128)(2,1)S(1)}, bf16[2,5,32,5,32]{4,2,3,1,0:T(8,128)(2,1)}, u32[]{:S(2)}) copy-start(bf16[2,5,32,5,32]{4,2,3,1,0:T(8,128)(2,1)} %param.12) | copy-start | bytes 307204
  2.0 79.9 %collective-permute-start.1 = (bf16[8,5,32,128]{3,2,1,0:T(8,128)(2,1)}, bf16[8,5,32,128]{3,2,1,0:T(8,128)(2,1)}, u32[]{:S(2)}, u32[]{:S(2)}) collective-permute-start(bf16[8,5,32,128]{3,2,1,0:T(8,128)(2,1)} %convert_element_type.98), channel_id=1, source_target_pairs={{0,48},{16,64},{32,80},{48,96},{64,112},{80,128},{96,144},{112,160... | collective-permute-start | bytes 983048 | tf_op jit(solution)/shard_map/ppermute | solution.py:14
  10.1 74.0 %collective-permute-start.2 = (bf16[8,5,32,128]{3,2,1,0:T(8,128)(2,1)}, bf16[8,5,32,128]{3,2,1,0:T(8,128)(2,1)}, u32[]{:S(2)}, u32[]{:S(2)}) collective-permute-start(bf16[8,5,32,128]{3,2,1,0:T(8,128)(2,1)} %convert_element_type.98), channel_id=1, source_target_pairs={{0,32},{16,48},{32,64},{48,80},{64,96},{80,112},{96,128},{112,144}... | collective-permute-start | bytes 983048 | tf_op jit(solution)/shard_map/ppermute | solution.py:14
  15.0 70.2 %collective-permute-start.3 = (bf16[8,5,32,128]{3,2,1,0:T(8,128)(2,1)}, bf16[8,5,32,128]{3,2,1,0:T(8,128)(2,1)S(1)}, u32[]{:S(2)}, u32[]{:S(2)}) collective-permute-start(bf16[8,5,32,128]{3,2,1,0:T(8,128)(2,1)} %convert_element_type.98), channel_id=1, source_target_pairs={{0,16},{16,32},{32,48},{48,64},{64,80},{80,96},{96,112},{112,128},... | collective-permute-start | bytes 983048 | tf_op jit(solution)/shard_map/ppermute | solution.py:14
  17.9 67.5 %collective-permute-start.4 = (bf16[8,5,32,128]{3,2,1,0:T(8,128)(2,1)}, bf16[8,5,32,128]{3,2,1,0:T(8,128)(2,1)S(1)}, u32[]{:S(2)}, u32[]{:S(2)}) collective-permute-start(bf16[8,5,32,128]{3,2,1,0:T(8,128)(2,1)} %convert_element_type.98), channel_id=1, source_target_pairs={{16,0},{32,16},{48,32},{64,48},{80,64},{96,80},{112,96},{128,112},... | collective-permute-start | bytes 983048 | tf_op jit(solution)/shard_map/ppermute | solution.py:14
  21.3 58.7 %collective-permute-start = (f32[8,5,128]{2,0,1:T(8,128)S(1)}, f32[8,5,128]{2,0,1:T(8,128)S(1)}, u32[]{:S(2)}, u32[]{:S(2)}) collective-permute-start(f32[8,5,128]{2,0,1:T(8,128)S(1)} %bitcast.379), channel_id=1, source_target_pairs={{1,0},{2,1},{3,2},{4,3},{5,4},{6,5},{7,6},{8,7},{9,8},{10,9},{11,1... | collective-permute-start | bytes 61448 | tf_op jit(solution)/shard_map/ppermute | solution.py:14
  43.5 41.8 %copy-start = (f32[8,5,32,128]{3,2,1,0:T(8,128)S(1)}, f32[8,5,32,128]{3,2,1,0:T(8,128)}, u32[]{:S(2)}) copy-start(f32[8,5,32,128]{3,2,1,0:T(8,128)} %param.11) | copy-start | bytes 1966084
  79.9 15.7 %collective-permute-start.5 = (bf16[8,5,32,128]{3,2,1,0:T(8,128)(2,1)}, bf16[8,5,32,128]{3,2,1,0:T(8,128)(2,1)S(1)}, u32[]{:S(2)}, u32[]{:S(2)}) collective-permute-start(bf16[8,5,32,128]{3,2,1,0:T(8,128)(2,1)} %convert_element_type.98), channel_id=1, source_target_pairs={{32,0},{48,16},{64,32},{80,48},{96,64},{112,80},{128,96},{144,112}... | collective-permute-start | bytes 983048 | tf_op jit(solution)/shard_map/ppermute | solution.py:14
  81.9 40.8 %collective-permute-start.6 = (bf16[8,5,32,128]{3,2,1,0:T(8,128)(2,1)}, bf16[8,5,32,128]{3,2,1,0:T(8,128)(2,1)S(1)}, u32[]{:S(2)}, u32[]{:S(2)}) collective-permute-start(bf16[8,5,32,128]{3,2,1,0:T(8,128)(2,1)} %convert_element_type.98), channel_id=1, source_target_pairs={{48,0},{64,16},{80,32},{96,48},{112,64},{128,80},{144,96},{160,112... | collective-permute-start | bytes 983048 | tf_op jit(solution)/shard_map/ppermute | solution.py:14
  165.3 15.5 %collective-permute-start.7 = (f32[8,5,128]{2,0,1:T(8,128)S(1)}, f32[8,5,128]{2,0,1:T(8,128)S(1)}, u32[]{:S(2)}, u32[]{:S(2)}) collective-permute-start(f32[8,5,128]{2,0,1:T(8,128)S(1)} %bitcast.380), channel_id=1, source_target_pairs={{1,0},{2,1},{3,2},{4,3},{5,4},{6,5},{7,6},{8,7},{9,8},{10,9},{11,1... | collective-permute-start | bytes 61448 | tf_op jit(solution)/shard_map/ppermute | solution.py:14
  167.4 28.8 %collective-permute-start.8 = (bf16[8,5,32,128]{3,2,1,0:T(8,128)(2,1)S(1)}, bf16[8,5,32,128]{3,2,1,0:T(8,128)(2,1)S(1)}, u32[]{:S(2)}, u32[]{:S(2)}) collective-permute-start(bf16[8,5,32,128]{3,2,1,0:T(8,128)(2,1)S(1)} %get-tuple-element.389), channel_id=1, source_target_pairs={{0,48},{16,64},{32,80},{48,96},{64,112},{80,128},{96,144},{112,160... | collective-permute-start | bytes 983048 | tf_op jit(solution)/shard_map/ppermute | solution.py:14
  171.1 35.8 %collective-permute-start.9 = (bf16[8,5,32,128]{3,2,1,0:T(8,128)(2,1)S(1)}, bf16[8,5,32,128]{3,2,1,0:T(8,128)(2,1)S(1)}, u32[]{:S(2)}, u32[]{:S(2)}) collective-permute-start(bf16[8,5,32,128]{3,2,1,0:T(8,128)(2,1)S(1)} %get-tuple-element.389), channel_id=1, source_target_pairs={{0,32},{16,48},{32,64},{48,80},{64,96},{80,112},{96,128},{112,144}... | collective-permute-start | bytes 983048 | tf_op jit(solution)/shard_map/ppermute | solution.py:14
  175.5 40.2 %collective-permute-start.10 = (bf16[8,5,32,128]{3,2,1,0:T(8,128)(2,1)S(1)}, bf16[8,5,32,128]{3,2,1,0:T(8,128)(2,1)S(1)}, u32[]{:S(2)}, u32[]{:S(2)}) collective-permute-start(bf16[8,5,32,128]{3,2,1,0:T(8,128)(2,1)S(1)} %get-tuple-element.389), channel_id=1, source_target_pairs={{0,16},{16,32},{32,48},{48,64},{64,80},{80,96},{96,112},{112,128},... | collective-permute-start | bytes 983048 | tf_op jit(solution)/shard_map/ppermute | solution.py:14
  177.5 38.3 %collective-permute-start.11 = (bf16[8,5,32,128]{3,2,1,0:T(8,128)(2,1)S(1)}, bf16[8,5,32,128]{3,2,1,0:T(8,128)(2,1)S(1)}, u32[]{:S(2)}, u32[]{:S(2)}) collective-permute-start(bf16[8,5,32,128]{3,2,1,0:T(8,128)(2,1)S(1)} %get-tuple-element.389), channel_id=1, source_target_pairs={{16,0},{32,16},{48,32},{64,48},{80,64},{96,80},{112,96},{128,112},... | collective-permute-start | bytes 983048 | tf_op jit(solution)/shard_map/ppermute | solution.py:14
  180.8 35.0 %collective-permute-start.12 = (bf16[8,5,32,128]{3,2,1,0:T(8,128)(2,1)S(1)}, bf16[8,5,32,128]{3,2,1,0:T(8,128)(2,1)S(1)}, u32[]{:S(2)}, u32[]{:S(2)}) collective-permute-start(bf16[8,5,32,128]{3,2,1,0:T(8,128)(2,1)S(1)} %get-tuple-element.389), channel_id=1, source_target_pairs={{32,0},{48,16},{64,32},{80,48},{96,64},{112,80},{128,96},{144,112}... | collective-permute-start | bytes 983048 | tf_op jit(solution)/shard_map/ppermute | solution.py:14
  196.2 29.7 %collective-permute-start.13 = (bf16[8,5,32,128]{3,2,1,0:T(8,128)(2,1)S(1)}, bf16[8,5,32,128]{3,2,1,0:T(8,128)(2,1)S(1)}, u32[]{:S(2)}, u32[]{:S(2)}) collective-permute-start(bf16[8,5,32,128]{3,2,1,0:T(8,128)(2,1)S(1)} %get-tuple-element.389), channel_id=1, source_target_pairs={{48,0},{64,16},{80,32},{96,48},{112,64},{128,80},{144,96},{160,112... | collective-permute-start | bytes 983048 | tf_op jit(solution)/shard_map/ppermute | solution.py:14
where the time goes:
time: 269 us; the launch traced here: 268 us
  waiting for transfers between devices  78.5 us (29%)
  blocking collectives  74 us (28%)
  starting transfers between devices  42.7 us (16%)
  matrix products  29.2 us (11%)
  other arithmetic  20.6 us (8%)
  local copies, waits for them, and re-layouts  11.5 us (4%)
  between operations  10.6 us (4%)
    ppermute x14, waiting for transfers between devices, passed_along(): lax.ppermute(value, axis, [(source, source + steps) for source in range(f...  78.5 us
    all_gather x4, blocking collectives, prefix_2(): pieces = jax.tree.map(lambda part: lax.all_gather(part, axis), value)  74 us
    ppermute x14, starting transfers between devices, passed_along(): lax.ppermute(value, axis, [(source, source + steps) for source in range(f...  42.7 us
    dot_general x30, matrix products, edge_mix(): jnp.einsum('vw,mwc->mvc', map_imag, vec_imag, precision=high)  7.11 us
    dot_general x30, matrix products, edge_mix(): jnp.einsum('vw,mwc->mvc', map_real, vec_imag, precision=high)  6.8 us
    convert_element_type x4, other arithmetic, body(): forced = complex_apply(precond, mixing.astype(jnp.bfloat16))  5.69 us
  transfers between devices with their start and end apart: 14, of which 6 were waited for; matrix products, arithmetic and copies ran while one was open for 5% of the time, Pallas kernels for 0%

commit v1 on v0

v1 whole, which is shorter than its diff:
```python
import functools

import jax
import jax.numpy as jnp
from jax import lax
from jax.experimental import pallas as pl
from jax.experimental.pallas import tpu as pltpu
from jax.sharding import PartitionSpec as P

NH = 8
HSTEP = 6
ITERS = 2
HALF = NH // 2
OFFS = [HSTEP * (k - HALF) if k < HALF else HSTEP * (k - HALF + 1) for k in range(NH)]
HOPS = 3
CHUNKS = 2
MESH = pl.DeviceIdType.MESH


def kernel(
    n_mode, n_slab,
    edge_ref, rhs_ref, start_ref, mat_ref, coef_ref, out_ref,
    frozen, halo, coef_b, col_b, trans, tails, rows_out, rows_in,
    base, acc_a, acc_b, mixed, edge_v, edge_j,
    halo_send, halo_recv, trans_send, trans_recv, tail_send, tail_recv, row_send, row_recv,
):
    modes = rhs_ref.shape[0]
    nrow = rhs_ref.shape[1]
    nvar = edge_ref.shape[0]
    rad = nrow // nvar
    part = modes // CHUNKS
    me = lax.axis_index("mode")
    slab = lax.axis_index("slab")
    lane = lax.broadcasted_iota(jnp.int32, (1, 128), 1)
    sign = jnp.where(lane < 64, -1.0, 1.0).astype(jnp.float32)

    def turn(x):
        return pltpu.roll(x, 64, x.ndim - 1) * sign

    barrier = pltpu.get_barrier_semaphore()
    for other in range(n_slab):
        @pl.when(other != slab)
        def _():
            pl.semaphore_signal(barrier, inc=1, device_id={"slab": other}, device_id_type=MESH)

    @pl.when(me > 0)
    def _():
        pl.semaphore_signal(barrier, inc=1, device_id={"mode": me - 1}, device_id_type=MESH)

    @pl.when(me < n_mode - 1)
    def _():
        pl.semaphore_signal(barrier, inc=1, device_id={"mode": me + 1}, device_id_type=MESH)

    frozen[0] = start_ref[...].astype(jnp.bfloat16)
    for v in range(nvar):
        rows_out[0, v] = start_ref[:, v * rad, :]

    n_near = jnp.where(me > 0, 1, 0) + jnp.where(me < n_mode - 1, 1, 0)
    pl.semaphore_wait(barrier, n_slab - 1 + n_near)

    def halo_copy(it, way, hop, c):
        cut = pl.ds(c * part, part)
        src = frozen.at[it, cut] if hop == 0 else halo.at[it, way, hop - 1, cut]
        to = me + 1 if way == 0 else me - 1
        return pltpu.make_async_remote_copy(
            src_ref=src,
            dst_ref=halo.at[it, way, hop, cut],
            send_sem=halo_send.at[it, way, hop, c],
            recv_sem=halo_recv.at[it, way, hop, c],
            device_id={"mode": to},
            device_id_type=MESH,
        )

    def sends(way, hop):
        if way == 0:
            return (me < n_mode - 1) & (me >= hop)
        return (me > 0) & (me + hop < n_mode)

    def gets(way, hop):
        return me >= hop + 1 if way == 0 else me + hop + 1 < n_mode

    def halo_start(it, hop, c):
        for way in range(2):
            @pl.when(sends(way, hop))
            def _():
                halo_copy(it, way, hop, c).start()

    def halo_wait(it, hop, c):
        for way in range(2):
            @pl.when(gets(way, hop))
            def _():
                halo_copy(it, way, hop, c).wait_recv()

    def row_copy(it):
        return pltpu.make_async_remote_copy(
            src_ref=rows_out.at[it], dst_ref=rows_in.at[it],
            send_sem=row_send.at[it], recv_sem=row_recv.at[it],
            device_id={"slab": slab - 1}, device_id_type=MESH,
        )

    def trans_copy(source, other):
        return pltpu.make_async_remote_copy(
            src_ref=trans.at[source], dst_ref=trans.at[source],
            send_sem=trans_send.at[other], recv_sem=trans_recv.at[source],
            device_id={"slab": other}, device_id_type=MESH,
        )

    def tail_copy(it, source, other):
        return pltpu.make_async_remote_copy(
            src_ref=tails.at[it, source], dst_ref=tails.at[it, source],
            send_sem=tail_send.at[it, other], recv_sem=tail_recv.at[it, source],
            device_id={"slab": other}, device_id_type=MESH,
        )

    for c in range(CHUNKS):
        halo_start(0, 0, c)

    @pl.when(slab > 0)
    def _():
        row_copy(0).start()

    for v in range(nvar):
        for p in range(2):
            col = mat_ref[p * nrow:(p + 1) * nrow, v * rad:v * rad + 1].astype(jnp.float32)
            col_b[p, v] = jnp.broadcast_to(col * edge_ref[v, 0], (nrow, 128))
    for p in range(2):
        for v in range(nvar):
            for w in range(nvar):
                row = v * rad + rad - 1
                trans[slab, pl.ds(p * nvar * nvar + v * nvar + w, 1)] = -col_b[p, w, row:row + 1, :]
    for other in range(1, n_slab):
        @pl.when(other > slab)
        def _():
            trans_copy(slab, other).start()
    for p in range(2):
        for k in range(NH):
            pick = coef_ref[:, p * NH + k:p * NH + k + 1]
            coef_b[p, k] = jnp.broadcast_to(pick, (nrow, 128))
    for it in range(ITERS):
        for hop in range(HOPS):
            for way in range(2):
                @pl.when(jnp.logical_not(gets(way, hop)))
                def _():
                    halo[it, way, hop] = jnp.zeros(halo.shape[3:], halo.dtype)

    @pl.when(slab == n_slab - 1)
    def _():
        rows_in[...] = jnp.zeros_like(rows_in)

    def product(x):
        both = jnp.dot(mat_ref[...], x, preferred_element_type=jnp.float32)
        return both[:nrow] + turn(both[nrow:])

    def accumulate(it, stage):
        def block(v, carry):
            cut = pl.ds(pl.multiple_of(v * rad, rad), rad)
            for m in range(modes):
                a = b = None
                if stage > 1:
                    a, b = acc_a[m, cut], acc_b[m, cut]
                for k in range(NH):
                    dist, src = divmod(m - OFFS[k], modes)
                    if max(1, abs(dist)) != stage:
                        continue
                    if dist == 0:
                        x = frozen[it, src, cut]
                    else:
                        x = halo[it, 0 if dist < 0 else 1, abs(dist) - 1, src, cut]
                    x = x.astype(jnp.float32)
                    ax, bx = coef_b[0, k, cut] * x, coef_b[1, k, cut] * x
                    a = ax if a is None else a + ax
                    b = bx if b is None else b + bx
                if stage == HOPS:
                    mixed[m, cut] = (a + turn(b)).astype(jnp.bfloat16)
                else:
                    acc_a[m, cut] = a
                    acc_b[m, cut] = b
            return carry

        lax.fori_loop(0, nvar, block, 0)

    last = lax.broadcasted_iota(jnp.int32, (rad, 1), 0) == rad - 1

    for it in range(ITERS):
        @pl.when(slab < n_slab - 1)
        def _():
            row_copy(it).wait_recv()

        for m in range(modes):
            pieces = []
            for v in range(nvar):
                x = rhs_ref[m, v * rad:(v + 1) * rad, :]
                nxt = edge_ref[v, rad - 1] * rows_in[it, v, m:m + 1, :]
                pieces.append(jnp.where(last, x + nxt, x).astype(jnp.bfloat16))
            base[m] = product(jnp.concatenate(pieces, axis=0))

        for hop in range(HOPS):
            for c in range(CHUNKS):
                halo_wait(it, hop, c)
                if hop + 1 < HOPS:
                    halo_start(it, hop + 1, c)
            accumulate(it, hop + 1)

        for m in range(modes):
            base[m] = base[m] - product(mixed[m])
        for v in range(nvar):
            tails[it, slab, v] = base[:, v * rad + rad - 1, :]
        for other in range(n_slab - 1, 0, -1):
            @pl.when(other > slab)
            def _():
                tail_copy(it, slab, other).start()

        def carry_on(j, edge):
            if it == 0:
                trans_copy(j, slab).wait_recv()
            tail_copy(it, j, slab).wait_recv()
            turned = [turn(e) for e in edge]
            fresh = []
            for v in range(nvar):
                total = tails[it, j, v]
                for w in range(nvar):
                    at = v * nvar + w
                    total = total + trans[j, pl.ds(at, 1)] * edge[w]
                    total = total + trans[j, pl.ds(nvar * nvar + at, 1)] * turned[w]
                fresh.append(total)
            return tuple(fresh)

        zero = jnp.zeros((modes, 128), jnp.float32)
        edge = lax.fori_loop(0, slab, carry_on, (zero,) * nvar)
        for w in range(nvar):
            edge_v[w] = edge[w]
            edge_j[w] = turn(edge[w])
        for m in range(modes):
            total = base[m]
            for w in range(nvar):
                total = total - col_b[0, w] * edge_v[w, m:m + 1, :]
                total = total - col_b[1, w] * edge_j[w, m:m + 1, :]
            if it == ITERS - 1:
                out_ref[m] = total
            else:
                frozen[it + 1, m] = total.astype(jnp.bfloat16)
                for v in range(nvar):
                    rows_out[it + 1, v, m:m + 1, :] = total[v * rad:v * rad + 1, :]
        if it < ITERS - 1:
            for c in range(CHUNKS):
                halo_start(it + 1, 0, c)

            @pl.when(slab > 0)
            def _():
                row_copy(it + 1).start()

    for other in range(1, n_slab):
        @pl.when(other > slab)
        def _():
            trans_copy(slab, other).wait_send()
            for it in range(ITERS):
                tail_copy(it, slab, other).wait_send()

    @pl.when(slab > 0)
    def _():
        for it in range(ITERS):
            row_copy(it).wait_send()

    for it in range(ITERS):
        for way in range(2):
            for hop in range(HOPS):
                @pl.when(sends(way, hop))
                def _():
                    for c in range(CHUNKS):
                        halo_copy(it, way, hop, c).wait_send()


def body(rhs, start_state, precond, coupling, edge_coef, harm_order):
    n_mode, n_slab = lax.axis_size("mode"), lax.axis_size("slab")
    modes, nvar, rad, cols = rhs.shape
    nrow = nvar * rad
    chosen = harm_order[None, :] == jnp.arange(NH)[:, None]
    ranked = jnp.sum(
        jnp.where(chosen[None, :, :, None, None], coupling[:, None], 0.0), axis=2
    )
    coefs = ranked.transpose(2, 3, 0, 1).reshape(nrow, 2 * NH)
    matrix = precond.reshape(2 * nrow, nrow)
    f32, bf16 = jnp.float32, jnp.bfloat16
    dma = pltpu.SemaphoreType.DMA
    vmem = pl.BlockSpec(memory_space=pltpu.VMEM)
    state = pl.pallas_call(
        functools.partial(kernel, n_mode, n_slab),
        out_shape=jax.ShapeDtypeStruct((modes, nrow, cols), f32),
        in_specs=[pl.BlockSpec(memory_space=pltpu.SMEM)] + [vmem] * 4,
        out_specs=vmem,
        scratch_shapes=[
            pltpu.VMEM((ITERS, modes, nrow, cols), bf16),
            pltpu.VMEM((ITERS, 2, HOPS, modes, nrow, cols), bf16),
            pltpu.VMEM((2, NH, nrow, 128), f32),
            pltpu.VMEM((2, nvar, nrow, 128), f32),
            pltpu.VMEM((n_slab, 56, 128), f32),
            pltpu.VMEM((ITERS, n_slab, nvar, modes, cols), f32),
            pltpu.VMEM((ITERS, nvar, modes, cols), f32),
            pltpu.VMEM((ITERS, nvar, modes, cols), f32),
            pltpu.VMEM((modes, nrow, cols), f32),
            pltpu.VMEM((modes, nrow, cols), f32),
            pltpu.VMEM((modes, nrow, cols), f32),
            pltpu.VMEM((modes, nrow, cols), bf16),
            pltpu.VMEM((nvar, modes, cols), f32),
            pltpu.VMEM((nvar, modes, cols), f32),
            dma((ITERS, 2, HOPS, CHUNKS)),
            dma((ITERS, 2, HOPS, CHUNKS)),
            dma((n_slab,)),
            dma((n_slab,)),
            dma((ITERS, n_slab)),
            dma((ITERS, n_slab)),
            dma((ITERS,)),
            dma((ITERS,)),
        ],
        compiler_params=pltpu.CompilerParams(
            collective_id=0, has_side_effects=True, vmem_limit_bytes=48 * 1024 * 1024
        ),
    )(edge_coef, rhs.reshape(modes, nrow, cols), start_state.reshape(modes, nrow, cols), matrix, coefs)
    return state.reshape(rhs.shape)


def solution(mesh):
    in_specs = (
        P("mode", None, "slab", None),
        P("mode", None, "slab", None),
        P(None, None, "slab", None, None),
        P(None, None, None, "slab"),
        P(None, "slab"),
        P(),
    )
    out_specs = P("mode", None, "slab", None)
    return jax.shard_map(body, mesh=mesh, in_specs=in_specs, out_specs=out_specs, check_vma=False)
```

time: 269 us -> 89.9 us (0.33)
  the two profiles are of different devices: /device:TPU:33 before, /device:TPU:494 now
where the time goes in v1:
time: 89.9 us; the launch traced here: 89.7 us
  Pallas kernels  84.6 us (94%)
  local copies, waits for them, and re-layouts  4.02 us (4%)
  other arithmetic  0.96 us (1%)
    pallas_call x1, Pallas kernels, body(): pl.pallas_call(functools.partial(kernel, n_mode, n_slab), out_shape=jax.S...  84.6 us
    unnamed x9, local copies, waits for them, and re-layouts  2.22 us

profile of v1, /device:TPU:494, one launch (start us, length us, event | category | flops | bytes accessed | tf_op | source)
XLA Modules:
  0.0 89.7 jit_solution(13276632495505639408)
XLA Ops:
  0.0 0.0 copy-start.3
  0.0 0.7 copy-done.3
  0.7 1.0 %select_reduce_fusion = f32[2,8,5,32]{3,2,1,0:T(8,128)S(1)} fusion(f32[2,8,5,32]{3,1,2,0:T(8,128)} %param.9, pred[8,8]{1,0:T(8,128)(4,1)S(1)} %iota_compare_fusion), kind=kLoop, calls=%fused_computation | loop fusion | flops 38400 | bytes 20544 | tf_op jit(solution)/shard_map/reduce_sum | solution.py:278
  1.6 0.1 reshape.40
  1.7 0.1 copy.15.coef_ref
  1.8 0.0 copy-start.1
  1.8 1.3 %copy.16 = bf16[2,5,32,5,32]{4,3,2,1,0:T(8,128)(2,1)S(1)} copy(bf16[2,5,32,5,32]{4,2,3,1,0:T(8,128)(2,1)} %param.8) | data formatting | bytes 204800 | tf_op jit(solution)/shard_map/reshape | solution.py:282
  3.1 0.0 copy-start
  3.1 0.0 copy-start.2
  3.1 0.3 reshape.42.mat_ref
  3.5 0.0 copy-done.1
  3.5 0.7 copy-done
  4.2 0.0 copy-done.2
  4.2 84.6 %shard_map.64 = f32[8,160,128]{2,1,0:T(8,128)S(1)} custom-call(f32[5,32]{1,0:T(8,128)S(1)} %copy-done.2, f32[8,160,128]{2,1,0:T(8,128)S(1)} %bitcast.7, f32[8,160,128]{2,1,0:T(8,128)S(1)} %bitcast.8, bf16[320,160]{1,0:T(8,128)(2,1)S(1)} %reshape.42.mat_ref, f32[160,16]{1,0:T(8,128)S(1)} %copy.15.coef_ref), custom_call_target="tpu_custom_call" | custom-call | tf_op jit(solution)/shard_map/pallas_call | solution.py:286
  88.8 0.8 copy.19
  (1 shorter events, 0.0 us)
Async XLA Ops:
  0.0 0.7 copy-start.3
  1.8 1.7 %copy-start.1 = (f32[8,5,32,128]{3,2,1,0:T(8,128)S(1)}, f32[8,5,32,128]{3,2,1,0:T(8,128)}, u32[]{:S(2)}) copy-start(f32[8,5,32,128]{3,2,1,0:T(8,128)} %param.7) | copy-start | bytes 1966084
  3.1 1.1 %copy-start = (f32[8,5,32,128]{3,2,1,0:T(8,128)S(1)}, f32[8,5,32,128]{3,2,1,0:T(8,128)}, u32[]{:S(2)}) copy-start(f32[8,5,32,128]{3,2,1,0:T(8,128)} %param.6) | copy-start | bytes 1966084
  3.1 1.1 %copy-start.2 = (f32[5,32]{1,0:T(8,128)S(1)}, f32[5,32]{1,0:T(8,128)}, u32[]{:S(2)}) copy-start(f32[5,32]{1,0:T(8,128)} %edge_ref.1) | copy-start | bytes 1924

commit v2 on v1

--- a/solution.py
+++ b/solution.py
@@ -13,7 +13,7 @@
 HALF = NH // 2
 OFFS = [HSTEP * (k - HALF) if k < HALF else HSTEP * (k - HALF + 1) for k in range(NH)]
 HOPS = 3
-CHUNKS = 2
+CHUNKS = 4
 MESH = pl.DeviceIdType.MESH
 
 
@@ -79,17 +79,15 @@
     def gets(way, hop):
         return me >= hop + 1 if way == 0 else me + hop + 1 < n_mode
 
-    def halo_start(it, hop, c):
-        for way in range(2):
-            @pl.when(sends(way, hop))
-            def _():
-                halo_copy(it, way, hop, c).start()
-
-    def halo_wait(it, hop, c):
-        for way in range(2):
-            @pl.when(gets(way, hop))
-            def _():
-                halo_copy(it, way, hop, c).wait_recv()
+    def halo_start(it, hop, c, way):
+        @pl.when(sends(way, hop))
+        def _():
+            halo_copy(it, way, hop, c).start()
+
+    def halo_wait(it, hop, c, way):
+        @pl.when(gets(way, hop))
+        def _():
+            halo_copy(it, way, hop, c).wait_recv()
 
     def row_copy(it):
         return pltpu.make_async_remote_copy(
@@ -113,7 +111,8 @@
         )
 
     for c in range(CHUNKS):
-        halo_start(0, 0, c)
+        for way in range(2):
+            halo_start(0, 0, c, way)
 
     @pl.when(slab > 0)
     def _():
@@ -196,15 +195,16 @@
 
         for hop in range(HOPS):
             for c in range(CHUNKS):
-                halo_wait(it, hop, c)
-                if hop + 1 < HOPS:
-                    halo_start(it, hop + 1, c)
+                for way in range(2):
+                    halo_wait(it, hop, c, way)
+                    if hop + 1 < HOPS:
+                        halo_start(it, hop + 1, c, way)
             accumulate(it, hop + 1)
 
         for m in range(modes):
             base[m] = base[m] - product(mixed[m])
-        for v in range(nvar):
-            tails[it, slab, v] = base[:, v * rad + rad - 1, :]
+        ends = [base[:, v * rad + rad - 1, :] for v in range(nvar)]
+        tails[it, slab] = jnp.concatenate(ends, axis=0).astype(jnp.bfloat16)
         for other in range(n_slab - 1, 0, -1):
             @pl.when(other > slab)
             def _():
@@ -216,8 +216,9 @@
             tail_copy(it, j, slab).wait_recv()
             turned = [turn(e) for e in edge]
             fresh = []
+            sent = tails[it, j].astype(jnp.float32)
             for v in range(nvar):
-                total = tails[it, j, v]
+                total = sent[v * modes:(v + 1) * modes]
                 for w in range(nvar):
                     at = v * nvar + w
                     total = total + trans[j, pl.ds(at, 1)] * edge[w]
@@ -241,10 +242,10 @@
                 frozen[it + 1, m] = total.astype(jnp.bfloat16)
                 for v in range(nvar):
                     rows_out[it + 1, v, m:m + 1, :] = total[v * rad:v * rad + 1, :]
+                if (m + 1) % part == 0:
+                    for way in range(2):
+                        halo_start(it + 1, 0, m // part, way)
         if it < ITERS - 1:
-            for c in range(CHUNKS):
-                halo_start(it + 1, 0, c)
-
             @pl.when(slab > 0)
             def _():
                 row_copy(it + 1).start()
@@ -294,7 +295,7 @@
             pltpu.VMEM((2, NH, nrow, 128), f32),
             pltpu.VMEM((2, nvar, nrow, 128), f32),
             pltpu.VMEM((n_slab, 56, 128), f32),
-            pltpu.VMEM((ITERS, n_slab, nvar, modes, cols), f32),
+            pltpu.VMEM((ITERS, n_slab, nvar * modes, cols), bf16),
             pltpu.VMEM((ITERS, nvar, modes, cols), f32),
             pltpu.VMEM((ITERS, nvar, modes, cols), f32),
             pltpu.VMEM((modes, nrow, cols), f32),

time: 89.9 us -> 79.4 us (0.88)
  the two profiles are of different devices: /device:TPU:494 before, /device:TPU:31 now
where the time goes in v2:
time: 79.4 us; the launch traced here: 79.2 us
  Pallas kernels  74.1 us (93%)
  local copies, waits for them, and re-layouts  4.02 us (5%)
  other arithmetic  0.96 us (1%)
    pallas_call x1, Pallas kernels, body(): pl.pallas_call(functools.partial(kernel, n_mode, n_slab), out_shape=jax.S...  74.1 us
    unnamed x9, local copies, waits for them, and re-layouts  2.22 us
    reshape x2, local copies, waits for them, and re-layouts, body(): matrix = precond.reshape(2 * nrow, nrow)  1.62 us

profile of v2, /device:TPU:31, one launch (start us, length us, event | category | flops | bytes accessed | tf_op | source)
XLA Modules:
  0.0 79.2 jit_solution(5019294712104022858)
XLA Ops:
  0.0 0.0 copy-start.3
  0.0 0.7 copy-done.3
  0.7 1.0 %select_reduce_fusion = f32[2,8,5,32]{3,2,1,0:T(8,128)S(1)} fusion(f32[2,8,5,32]{3,1,2,0:T(8,128)} %param.9, pred[8,8]{1,0:T(8,128)(4,1)S(1)} %iota_compare_fusion), kind=kLoop, calls=%fused_computation | loop fusion | flops 38400 | bytes 20544 | tf_op jit(solution)/shard_map/reduce_sum | solution.py:279
  1.6 0.1 reshape.40
  1.7 0.1 copy.15.coef_ref
  1.8 0.0 copy-start.1
  1.8 1.3 %copy.16 = bf16[2,5,32,5,32]{4,3,2,1,0:T(8,128)(2,1)S(1)} copy(bf16[2,5,32,5,32]{4,2,3,1,0:T(8,128)(2,1)} %param.8) | data formatting | bytes 204800 | tf_op jit(solution)/shard_map/reshape | solution.py:283
  3.1 0.0 copy-start
  3.1 0.0 copy-start.2
  3.1 0.3 reshape.42.mat_ref
  3.5 0.0 copy-done.1
  3.5 0.7 copy-done
  4.2 0.0 copy-done.2
  4.2 74.1 %shard_map.64 = f32[8,160,128]{2,1,0:T(8,128)S(1)} custom-call(f32[5,32]{1,0:T(8,128)S(1)} %copy-done.2, f32[8,160,128]{2,1,0:T(8,128)S(1)} %bitcast.7, f32[8,160,128]{2,1,0:T(8,128)S(1)} %bitcast.8, bf16[320,160]{1,0:T(8,128)(2,1)S(1)} %reshape.42.mat_ref, f32[160,16]{1,0:T(8,128)S(1)} %copy.15.coef_ref), custom_call_target="tpu_custom_call" | custom-call | tf_op jit(solution)/shard_map/pallas_call | solution.py:287
  78.3 0.8 %copy.19 = f32[8,5,32,128]{3,2,1,0:T(8,128)} copy(f32[8,5,32,128]{3,2,1,0:T(8,128)S(1)} %bitcast.6) | data formatting | bytes 1310720
  (1 shorter events, 0.0 us)
Async XLA Ops:
  0.0 0.7 copy-start.3
  1.8 1.7 %copy-start.1 = (f32[8,5,32,128]{3,2,1,0:T(8,128)S(1)}, f32[8,5,32,128]{3,2,1,0:T(8,128)}, u32[]{:S(2)}) copy-start(f32[8,5,32,128]{3,2,1,0:T(8,128)} %param.7) | copy-start | bytes 1966084
  3.1 1.1 %copy-start = (f32[8,5,32,128]{3,2,1,0:T(8,128)S(1)}, f32[8,5,32,128]{3,2,1,0:T(8,128)}, u32[]{:S(2)}) copy-start(f32[8,5,32,128]{3,2,1,0:T(8,128)} %param.6) | copy-start | bytes 1966084
  3.1 1.1 %copy-start.2 = (f32[5,32]{1,0:T(8,128)S(1)}, f32[5,32]{1,0:T(8,128)}, u32[]{:S(2)}) copy-start(f32[5,32]{1,0:T(8,128)} %edge_ref.1) | copy-start | bytes 1924

commit v3 on v2

--- a/solution.py
+++ b/solution.py
@@ -55,6 +55,15 @@
     for v in range(nvar):
         rows_out[0, v] = start_ref[:, v * rad, :]
 
+    for v in range(nvar):
+        for p in range(2):
+            col = mat_ref[p * nrow:(p + 1) * nrow, v * rad:v * rad + 1].astype(jnp.float32)
+            col_b[p, v] = jnp.broadcast_to(col * edge_ref[v, 0], (nrow, 128))
+    for p in range(2):
+        for k in range(NH):
+            pick = coef_ref[:, p * NH + k:p * NH + k + 1]
+            coef_b[p, k] = jnp.broadcast_to(pick, (nrow, 128))
+
     n_near = jnp.where(me > 0, 1, 0) + jnp.where(me < n_mode - 1, 1, 0)
     pl.semaphore_wait(barrier, n_slab - 1 + n_near)
 
@@ -118,10 +127,6 @@
     def _():
         row_copy(0).start()
 
-    for v in range(nvar):
-        for p in range(2):
-            col = mat_ref[p * nrow:(p + 1) * nrow, v * rad:v * rad + 1].astype(jnp.float32)
-            col_b[p, v] = jnp.broadcast_to(col * edge_ref[v, 0], (nrow, 128))
     for p in range(2):
         for v in range(nvar):
             for w in range(nvar):
@@ -131,10 +136,6 @@
         @pl.when(other > slab)
         def _():
             trans_copy(slab, other).start()
-    for p in range(2):
-        for k in range(NH):
-            pick = coef_ref[:, p * NH + k:p * NH + k + 1]
-            coef_b[p, k] = jnp.broadcast_to(pick, (nrow, 128))
     for it in range(ITERS):
         for hop in range(HOPS):
             for way in range(2):
@@ -214,23 +215,26 @@
             if it == 0:
                 trans_copy(j, slab).wait_recv()
             tail_copy(it, j, slab).wait_recv()
-            turned = [turn(e) for e in edge]
-            fresh = []
+            edge, turned = edge[:nvar], edge[nvar:]
+            fresh, fresh_turned = [], []
             sent = tails[it, j].astype(jnp.float32)
             for v in range(nvar):
                 total = sent[v * modes:(v + 1) * modes]
+                total_turned = turn(total)
                 for w in range(nvar):
                     at = v * nvar + w
-                    total = total + trans[j, pl.ds(at, 1)] * edge[w]
-                    total = total + trans[j, pl.ds(nvar * nvar + at, 1)] * turned[w]
+                    real, imag = trans[j, pl.ds(at, 1)], trans[j, pl.ds(nvar * nvar + at, 1)]
+                    total = total + (real * edge[w] + imag * turned[w])
+                    total_turned = total_turned + (real * turned[w] - imag * edge[w])
                 fresh.append(total)
-            return tuple(fresh)
+                fresh_turned.append(total_turned)
+            return tuple(fresh + fresh_turned)
 
         zero = jnp.zeros((modes, 128), jnp.float32)
-        edge = lax.fori_loop(0, slab, carry_on, (zero,) * nvar)
+        edge = lax.fori_loop(0, slab, carry_on, (zero,) * (2 * nvar))
         for w in range(nvar):
             edge_v[w] = edge[w]
-            edge_j[w] = turn(edge[w])
+            edge_j[w] = edge[nvar + w]
         for m in range(modes):
             total = base[m]
             for w in range(nvar):

time: 79.4 us -> 79.4 us (level)
  no operation moved by 1% of the time
where the time goes in v3:
time: 79.4 us; the launch traced here: 79.2 us
  Pallas kernels  74.1 us (93%)
  local copies, waits for them, and re-layouts  4.02 us (5%)
  other arithmetic  0.96 us (1%)
    pallas_call x1, Pallas kernels, body(): pl.pallas_call(functools.partial(kernel, n_mode, n_slab), out_shape=jax.S...  74.1 us
    unnamed x9, local copies, waits for them, and re-layouts  2.22 us
    reshape x2, local copies, waits for them, and re-layouts, body(): matrix = precond.reshape(2 * nrow, nrow)  1.62 us

profile of v3, /device:TPU:31, one launch (start us, length us, event | category | flops | bytes accessed | tf_op | source)
XLA Modules:
  0.0 79.2 jit_solution(12405817029109345275)
XLA Ops:
  0.0 0.0 copy-start.3
  0.0 0.7 copy-done.3
  0.7 1.0 %select_reduce_fusion = f32[2,8,5,32]{3,2,1,0:T(8,128)S(1)} fusion(f32[2,8,5,32]{3,1,2,0:T(8,128)} %param.9, pred[8,8]{1,0:T(8,128)(4,1)S(1)} %iota_compare_fusion), kind=kLoop, calls=%fused_computation | loop fusion | flops 38400 | bytes 20544 | tf_op jit(solution)/shard_map/reduce_sum | solution.py:283
  1.6 0.1 reshape.40
  1.7 0.1 copy.15.coef_ref
  1.8 0.0 copy-start.1
  1.8 1.3 %copy.16 = bf16[2,5,32,5,32]{4,3,2,1,0:T(8,128)(2,1)S(1)} copy(bf16[2,5,32,5,32]{4,2,3,1,0:T(8,128)(2,1)} %param.8) | data formatting | bytes 204800 | tf_op jit(solution)/shard_map/reshape | solution.py:287
  3.1 0.0 copy-start
  3.1 0.0 copy-start.2
  3.1 0.3 reshape.42.mat_ref
  3.5 0.0 copy-done.1
  3.5 0.7 copy-done
  4.2 0.0 copy-done.2
  4.2 74.1 %shard_map.64 = f32[8,160,128]{2,1,0:T(8,128)S(1)} custom-call(f32[5,32]{1,0:T(8,128)S(1)} %copy-done.2, f32[8,160,128]{2,1,0:T(8,128)S(1)} %bitcast.7, f32[8,160,128]{2,1,0:T(8,128)S(1)} %bitcast.8, bf16[320,160]{1,0:T(8,128)(2,1)S(1)} %reshape.42.mat_ref, f32[160,16]{1,0:T(8,128)S(1)} %copy.15.coef_ref), custom_call_target="tpu_custom_call" | custom-call | tf_op jit(solution)/shard_map/pallas_call | solution.py:291
  78.3 0.8 %copy.19 = f32[8,5,32,128]{3,2,1,0:T(8,128)} copy(f32[8,5,32,128]{3,2,1,0:T(8,128)S(1)} %bitcast.6) | data formatting | bytes 1310720
  (1 shorter events, 0.0 us)
Async XLA Ops:
  0.0 0.7 copy-start.3
  1.8 1.7 %copy-start.1 = (f32[8,5,32,128]{3,2,1,0:T(8,128)S(1)}, f32[8,5,32,128]{3,2,1,0:T(8,128)}, u32[]{:S(2)}) copy-start(f32[8,5,32,128]{3,2,1,0:T(8,128)} %param.7) | copy-start | bytes 1966084
  3.1 1.1 %copy-start = (f32[8,5,32,128]{3,2,1,0:T(8,128)S(1)}, f32[8,5,32,128]{3,2,1,0:T(8,128)}, u32[]{:S(2)}) copy-start(f32[8,5,32,128]{3,2,1,0:T(8,128)} %param.6) | copy-start | bytes 1966084
  3.1 1.1 %copy-start.2 = (f32[5,32]{1,0:T(8,128)S(1)}, f32[5,32]{1,0:T(8,128)}, u32[]{:S(2)}) copy-start(f32[5,32]{1,0:T(8,128)} %edge_ref.1) | copy-start | bytes 1924
